TPU v7x, 32 devices: a whole 2x2x4 slice. The times are simulated.
32 devices in a mesh: virt: 8 (over z, x), pair: 4 (over y, core).
Axes of the slice: x: 2, y: 2, z: 4, core: 2. Of those that a mesh axis runs over, the one named last changes fastest.
Arguments:
- amplitudes: bfloat16 [8, 1024, 2, 1024], P('pair'), may hold values from -6 to 6
- integrals: bfloat16 [2, 512, 8, 65536], P(None, None, None, ('virt', 'pair')), may hold values from -0.125 to 0.125
- virt_counts: int32 [8], replicated, may hold values from 32 to 64, as said below
- pair_counts: int32 [8], replicated, may hold values from 512 to 1024, as said below
- pair_list: int32 [8, 1024, 2], P('pair'), may hold values from 0 to 99
- eps_occ: float32 [100], replicated, may hold values from -2 to -0.3
- eps_virt: float32 [512], replicated, may hold values from 0.3 to 4
Outputs:
- update: bfloat16 [8, 1024, 32768], P('pair', None, 'virt')
- pair_energy: float32 [8, 1024], P('pair', 'virt')
Inputs may be any that keep to these rules, and one draw needn't show every extreme that they name: virt_counts[0] = 64; every count is at least 32. `pair_counts`: some pair symmetry has exactly 1024 pairs; every count is at least 512.
All inputs are finite; a program needn't handle non-finite values.
Results may differ from a plain program's by a relative error of at most 0.001.
Values may be sent and summed in bfloat16 or wider, within the bound.
A program may use at most 192 MiB of HBM per device.

v0:
```python
import jax
import jax.numpy as jnp
from jax import lax
from jax.sharding import PartitionSpec as P

IRREPS = 8
NV = 512
BLK = 64
CS = 16
SLABS = 2


def pick_counts(irrep_ids, table):
    onehot = irrep_ids[..., None] == jnp.arange(table.shape[0], dtype=jnp.int32)
    return jnp.sum(jnp.where(onehot, table, 0), axis=-1)


def shards(amplitudes, integrals, virt_counts, pair_counts, pair_list, eps_occ, eps_virt):
    local_irreps = amplitudes.shape[0]
    rows = amplitudes.shape[1]
    width = amplitudes.shape[3]
    n_virt = lax.axis_size("virt")
    n_pair = lax.axis_size("pair")
    a_local = NV // n_virt
    irrep_ids = lax.axis_index("pair") * local_irreps + jnp.arange(local_irreps, dtype=jnp.int32)
    slots = jnp.arange(BLK, dtype=jnp.int32)
    live_d = slots[None, :] < pick_counts(irrep_ids, virt_counts)[:, None]
    dmask = jnp.tile(live_d, (1, CS)).astype(jnp.bfloat16)
    masked = amplitudes * dmask[:, None, None, :]
    ladder = jnp.zeros((local_irreps, rows, a_local, BLK), jnp.float32)
    for s in range(SLABS):
        piece = integrals[s]
        moved = lax.all_to_all(
            lax.all_to_all(piece, "virt", split_axis=0, concat_axis=2, tiled=True),
            "pair",
            split_axis=1,
            concat_axis=2,
            tiled=True,
        )
        moved = moved.reshape(a_local, local_irreps, n_pair, n_virt, -1)
        moved = jnp.transpose(moved, (0, 1, 3, 2, 4)).reshape(a_local, local_irreps, BLK, width)
        ladder = ladder + jnp.einsum(
            "hrk,ahsk->hras", masked[:, :, s, :], moved, preferred_element_type=jnp.float32
        )
    a_global = lax.axis_index("virt") * a_local + jnp.arange(a_local, dtype=jnp.int32)
    a_irrep = a_global // BLK
    a_slot = a_global % BLK
    live_a = a_slot < pick_counts(a_irrep, virt_counts)
    eps_a = lax.dynamic_slice_in_dim(eps_virt, lax.axis_index("virt") * a_local, a_local)
    b_irrep = jnp.bitwise_xor(a_irrep[None, :], irrep_ids[:, None])
    b_onehot = (b_irrep[..., None] == jnp.arange(IRREPS, dtype=jnp.int32)).astype(jnp.float32)
    eps_table = eps_virt.reshape(IRREPS, BLK)
    eps_b = jnp.einsum("hag,gs->has", b_onehot, eps_table, precision=lax.Precision.HIGHEST)
    live_b = slots[None, None, :] < pick_counts(b_irrep, virt_counts)[..., None]
    occ_onehot = pair_list[..., None] == jnp.arange(eps_occ.shape[0], dtype=jnp.int32)
    occ_terms = jnp.sum(jnp.where(occ_onehot, eps_occ, 0.0), axis=-1)
    occ = occ_terms[:, :, 0] + occ_terms[:, :, 1]
    live_rows = (
        jnp.arange(rows, dtype=jnp.int32)[None, :] < pick_counts(irrep_ids, pair_counts)[:, None]
    )
    denom = (eps_a[None, :, None] + eps_b)[:, None, :, :] - occ[:, :, None, None]
    live = live_rows[:, :, None, None] & live_a[None, None, :, None] & live_b[:, None, :, :]
    ratio = jnp.where(live, ladder / denom, jnp.zeros_like(ladder))
    update = ratio.astype(jnp.bfloat16).reshape(local_irreps, rows, a_local * BLK)
    partial_value = jnp.sum(ratio * ladder, axis=(2, 3)) / (NV * BLK)
    energy = lax.psum_scatter(partial_value, "virt", scatter_dimension=1, tiled=True)
    return (update, energy)


def solution(mesh):
    placed = (
        P("pair", None, None, None),
        P(None, None, None, ("virt", "pair")),
        P(),
        P(),
        P("pair", None, None),
        P(),
        P(),
    )
    return jax.shard_map(
        shards,
        mesh=mesh,
        in_specs=placed,
        out_specs=(P("pair", None, "virt"), P("pair", "virt")),
        check_vma=False,
    )
```

profile of v0, /device:TPU:0, one launch (start us, length us, event | category | flops | bytes accessed | tf_op | source)
XLA Modules:
  0.0 1328.9 jit_solution(8190828221373560222)
XLA Ops:
  7.2 18.4 %slice_bitcast_fusion = (bf16[512,8,2048]{2,1,0:T(8,128)(2,1)S(1)}, bf16[512,8,2048]{2,1,0:T(8,128)(2,1)}) fusion(bf16[2,512,8,2048]{3,2,1,0:T(8,128)(2,1)} %param.8), kind=kLoop, calls=%fused_computation.6 | loop fusion | bytes 67108864 | tf_op jit(solution)/shard_map/squeeze | solution.py:32
  25.6 370.0 %all_to_all.66 = bf16[512,8,2048]{2,1,0:T(8,128)(2,1)} all-to-all(bf16[512,8,2048]{2,1,0:T(8,128)(2,1)S(1)} %get-tuple-element.14), channel_id=1, replica_groups=mesh['virt'=8,'pair'=4] {'virt'}, dimensions={0} | all-to-all | bytes 33554432 | tf_op jit(solution)/shard_map/all_to_all | solution.py:34
  395.6 5.8 all-to-all-start
  401.3 18.7 %copy.53 = bf16[8,64,8,2048]{3,0,2,1:T(8,128)(2,1)} copy(bf16[8,64,8,2048]{3,2,1,0:T(8,128)(2,1)} %bitcast.65) | data formatting | bytes 33554432 | tf_op jit(solution)/shard_map/all_to_all | solution.py:34
  420.0 25.6 %all_to_all.58 = bf16[64,8,16384]{2,1,0:T(8,128)(2,1)} reshape(bf16[64,8,8,2048]{3,2,1,0:T(8,128)(2,1)} %bitcast.66) | data formatting | bytes 33554432 | tf_op jit(solution)/shard_map/all_to_all | solution.py:34
  445.6 18.5 %copy.38 = bf16[64,8,16384]{2,0,1:T(8,128)(2,1)} copy(bf16[64,8,16384]{2,1,0:T(8,128)(2,1)} %all_to_all.58) | data formatting | bytes 33554432 | tf_op jit(solution)/shard_map/all_to_all | solution.py:34
  464.1 299.2 %all-to-all-done = bf16[512,8,2048]{2,1,0:T(8,128)(2,1)} async-done(((bf16[512,8,2048]{2,1,0:T(8,128)(2,1)}), bf16[512,8,2048]{2,1,0:T(8,128)(2,1)}, u32[]{:S(2)}, u32[]{:S(2)}) %all-to-all-start) | async-done | bytes 16777248 | tf_op jit(solution)/shard_map/all_to_all | solution.py:34
  763.3 7.0 all-to-all-start.3
  770.2 18.7 %copy.54 = bf16[8,64,8,2048]{3,0,2,1:T(8,128)(2,1)} copy(bf16[8,64,8,2048]{3,2,1,0:T(8,128)(2,1)} %bitcast.4) | data formatting | bytes 33554432 | tf_op jit(solution)/shard_map/all_to_all | solution.py:34
  788.9 25.6 %all_to_all.51 = bf16[64,8,16384]{2,1,0:T(8,128)(2,1)} reshape(bf16[64,8,8,2048]{3,2,1,0:T(8,128)(2,1)} %bitcast.67) | data formatting | bytes 33554432 | tf_op jit(solution)/shard_map/all_to_all | solution.py:34
  814.5 18.5 %copy.34 = bf16[64,8,16384]{2,0,1:T(8,128)(2,1)} copy(bf16[64,8,16384]{2,1,0:T(8,128)(2,1)} %all_to_all.51) | data formatting | bytes 33554432 | tf_op jit(solution)/shard_map/all_to_all | solution.py:34
  833.0 0.0 copy-start.3
  833.1 120.2 %all-to-all-done.3 = bf16[64,8,16384]{2,0,1:T(8,128)(2,1)} async-done(((bf16[64,8,16384]{2,0,1:T(8,128)(2,1)}), bf16[64,8,16384]{2,0,1:T(8,128)(2,1)}, u32[]{:S(2)}, u32[]{:S(2)}) %all-to-all-start.3) | async-done | bytes 16777248 | tf_op jit(solution)/shard_map/all_to_all | solution.py:33
  953.2 7.0 all-to-all-start.1
  960.2 0.2 reduce-scatter.4.cloned.1.call-start
  960.5 0.0 copy-done.1
  960.5 0.1 reshape.192
  960.5 0.1 dynamic_slice.3
  960.6 0.0 copy-done.2
  960.6 0.0 copy-done.4
  960.6 0.2 select_reduce_fusion.3
  960.8 0.1 compare_convert_fusion
  960.9 0.1 convert_element_type.16
  961.0 0.9 fusion.2
  962.0 0.1 select_reduce_fusion.1
  962.0 0.1 broadcast_xor_fusion
  962.1 0.1 select_reduce_fusion
  962.2 0.1 iota_compare_fusion.3
  962.3 0.1 iota_compare_fusion
  962.4 0.2 convolution_add_fusion.1
  962.6 0.1 broadcast_and_fusion
  962.8 9.3 copy_multiply_fusion
  972.0 8.0 copy.39
  980.0 10.4 copy.48
  990.4 14.1 %copy.40 = bf16[64,2,8,4,2048]{4,3,2,0,1:T(4,128)(2,1)} copy(bf16[64,2,8,4,2048]{4,2,0,3,1:T(8,128)(2,1)S(1)} %bitcast.69) | data formatting | bytes 33554432 | tf_op jit(solution)/shard_map/transpose | solution.py:41
  1004.6 23.7 %reshape.187 = bf16[64,2,64,1024]{3,2,0,1:T(8,128)(2,1)} reshape(bf16[64,2,8,4,2048]{4,3,2,0,1:T(4,128)(2,1)} %copy.40) | data formatting | bytes 33554432 | tf_op jit(solution)/shard_map/reshape | solution.py:41
  1028.3 115.0 %all-to-all-done.1 = bf16[64,8,16384]{2,0,1:T(8,128)(2,1)} async-done(((bf16[64,8,16384]{2,0,1:T(8,128)(2,1)}), bf16[64,8,16384]{2,0,1:T(8,128)(2,1)}, u32[]{:S(2)}, u32[]{:S(2)}) %all-to-all-start.1) | async-done | bytes 16777248 | tf_op jit(solution)/shard_map/all_to_all | solution.py:33
  1143.2 8.0 copy.35
  1151.2 10.4 copy.47
  1161.7 14.1 %copy.36 = bf16[64,2,8,4,2048]{4,3,2,0,1:T(4,128)(2,1)} copy(bf16[64,2,8,4,2048]{4,2,0,3,1:T(8,128)(2,1)S(1)} %bitcast.71) | data formatting | bytes 33554432 | tf_op jit(solution)/shard_map/transpose | solution.py:41
  1175.8 23.7 %reshape.185 = bf16[64,2,64,1024]{3,2,0,1:T(8,128)(2,1)} reshape(bf16[64,2,8,4,2048]{4,3,2,0,1:T(4,128)(2,1)} %copy.36) | data formatting | bytes 33554432 | tf_op jit(solution)/shard_map/reshape | solution.py:41
  1199.5 26.7 %fusion.1 = f32[2,1024,64,64]{1,3,2,0:T(8,128)} fusion(bf16[64,2,64,1024]{3,2,0,1:T(8,128)(2,1)} %reshape.185, bf16[2,1024,2,1024]{3,1,0,2:T(8,128)(2,1)} %copy_multiply_fusion), kind=kOutput, calls=%fused_computation.11 | convolution fusion | flops 17179869184 | bytes 54525952 | tf_op jit(solution)/shard_map/hrk,ahsk->hras/dot_general | solution.py:42
  1226.2 32.0 %multiply_reduce_fusion = (f32[2,1024]{1,0:T(2,128)S(1)}, bf16[2,1024,64,64]{1,3,2,0:T(8,128)(2,1)}) fusion(f32[2,1024]{1,0:T(2,128)S(1)} %bitcast.75, f32[2,64,64]{2,1,0:T(8,128)S(1)} %convolution_add_fusion.1, pred[2,64,64]{2,1,0:T(8,128)(4,1)S(1)} %iota_compare_fusion, pred[2,1024,64]{1,2,0:T(8,128)(4,1)S(1)} %broadcast_and_fusion, ...), kind=kOutput, calls=%fused_computation | convolution fusion | flops 17246976000 | bytes 71491584 | tf_op jit(solution)/shard_map/hrk,ahsk->hras/dot_general | solution.py:42
  1258.2 1.0 copy.44
  1259.2 0.0 reduce-scatter.4.cloned.1.call-update
  1259.2 21.2 %copy.41 = bf16[2,1024,4096]{2,1,0:T(8,128)(2,1)} copy(bf16[2,1024,4096]{1,2,0:T(8,128)(2,1)} %bitcast.72) | data formatting | bytes 33554432
  1280.5 40.1 %reduce-scatter.4.cloned.1.call-done = f32[128,2]{1,0:T(8,128)} async-done(((f32[1024,2]{1,0:T(8,128)}), f32[128,2]{1,0:T(8,128)}) %reduce-scatter.4.cloned.1.call-update) | async-done | bytes 1040
  1320.6 1.5 copy.45
  (13 shorter events, 0.1 us)
Async XLA Ops:
  395.6 367.7 %all-to-all-start = ((bf16[512,8,2048]{2,1,0:T(8,128)(2,1)}), bf16[512,8,2048]{2,1,0:T(8,128)(2,1)}, u32[]{:S(2)}, u32[]{:S(2)}) async-start(bf16[512,8,2048]{2,1,0:T(8,128)(2,1)} %get-tuple-element.15), calls=%async_computation | async-start | bytes 33554432 | tf_op jit(solution)/shard_map/all_to_all | solution.py:34
  763.3 190.0 %all-to-all-start.3 = ((bf16[64,8,16384]{2,0,1:T(8,128)(2,1)}), bf16[64,8,16384]{2,0,1:T(8,128)(2,1)}, u32[]{:S(2)}, u32[]{:S(2)}) async-start(bf16[64,8,16384]{2,0,1:T(8,128)(2,1)} %copy.38), calls=%async_computation.3 | async-start | bytes 33554432 | tf_op jit(solution)/shard_map/all_to_all | solution.py:33
  833.0 127.4 %copy-start.1 = (f32[512]{0:T(512)S(1)}, f32[512]{0:T(512)}, u32[]{:S(2)}) copy-start(f32[512]{0:T(512)} %param.13) | copy-start | bytes 6148
  833.0 127.6 %copy-start.2 = (s32[8]{0:T(128)S(1)}, s32[8]{0:T(128)}, u32[]{:S(2)}) copy-start(s32[8]{0:T(128)} %param.9) | copy-start | bytes 100
  833.0 127.6 %copy-start.4 = (s32[8]{0:T(128)S(1)}, s32[8]{0:T(128)}, u32[]{:S(2)}) copy-start(s32[8]{0:T(128)} %param.10) | copy-start | bytes 100
  833.0 127.9 %copy-start = (s32[2,1024,2]{1,2,0:T(2,128)S(1)}, s32[2,1024,2]{1,2,0:T(2,128)}, u32[]{:S(2)}) copy-start(s32[2,1024,2]{1,2,0:T(2,128)} %param.11) | copy-start | bytes 49156
  833.0 127.9 %copy-start.3 = (f32[100]{0:T(128)S(1)}, f32[100]{0:T(128)}, u32[]{:S(2)}) copy-start(f32[100]{0:T(128)} %param.12) | copy-start | bytes 1204
  953.2 190.0 %all-to-all-start.1 = ((bf16[64,8,16384]{2,0,1:T(8,128)(2,1)}), bf16[64,8,16384]{2,0,1:T(8,128)(2,1)}, u32[]{:S(2)}, u32[]{:S(2)}) async-start(bf16[64,8,16384]{2,0,1:T(8,128)(2,1)} %copy.34), calls=%async_computation.1 | async-start | bytes 33554432 | tf_op jit(solution)/shard_map/all_to_all | solution.py:33
  960.2 360.4 %reduce-scatter.4.cloned.1.call-start = ((), (), s32[]{:S(2)}) async-start(), calls=%async_computation.5 | async-start | bytes 589824
Sparse Core Ops, SparseCore 0:
  1259.4 61.1 reduce-scatter.3
where the time goes:
time: 1330 us
  waiting for transfers between devices  574 us (43%)
  blocking collectives  370 us (28%)
  local copies, waits for them, and re-layouts  280 us (21%)
  matrix products  59 us (4%)
  starting transfers between devices  19.9 us (1%)
  between operations  14.2 us (1%)
    all_to_all x1, blocking collectives, shards(): lax.all_to_all(piece, 'virt', split_axis=0, concat_axis=2, tiled=True)  370 us
    all_to_all x1, waiting for transfers between devices, shards(): lax.all_to_all(piece, 'virt', split_axis=0, concat_axis=2, tiled=True)  299 us
    all_to_all x2, waiting for transfers between devices, shards(): lax.all_to_all(lax.all_to_all(piece, 'virt', split_axis=0, concat_axis=2,...  235 us
    all_to_all x6, local copies, waits for them, and re-layouts, shards(): lax.all_to_all(piece, 'virt', split_axis=0, concat_axis=2, tiled=True)  126 us
    dot_general x2, matrix products, shards(): jnp.einsum('hrk,ahsk->hras', masked[:, :, s, :], moved, preferred_element...  58.7 us
    reshape x2, local copies, waits for them, and re-layouts, shards(): jnp.transpose(moved, (0, 1, 3, 2, 4))  47.4 us
    unnamed x16, local copies, waits for them, and re-layouts  44.6 us
    unnamed x2, waiting for transfers between devices  40.1 us
  transfers between devices with their start and end apart: 4, of which 4 were waited for; matrix products, arithmetic and copies ran while one was open for 12% of the time, Pallas kernels for 0%

commit v1 on v0

--- a/solution.py
+++ b/solution.py
@@ -31,7 +31,12 @@
     for s in range(SLABS):
         piece = integrals[s]
         moved = lax.all_to_all(
-            lax.all_to_all(piece, "virt", split_axis=0, concat_axis=2, tiled=True),
+            jnp.concatenate(
+                lax.all_to_all(
+                    jnp.stack(jnp.split(piece, lax.axis_size("virt"), axis=0)), "virt", 0, 0
+                ),
+                axis=2,
+            ),
             "pair",
             split_axis=1,
             concat_axis=2,

time: 1330 us -> 1350 us (1.015)
  waiting for transfers between devices: 574 us -> 612 us
  local copies, waits for them, and re-layouts: 280 us -> 257 us
    all_to_all x8 -> x2, local copies, waits for them, and re-layouts: 141 us -> 15.9 us  [shards(): lax.all_to_all(jnp.concatenate(lax.all_to_all(jnp.stack(jnp.split(piece,...]
    reshape x0 -> x4, local copies, waits for them, and re-layouts: none -> 88.5 us  [shards(): jnp.concatenate(lax.all_to_all(jnp.stack(jnp.split(piece, lax.axis_size('...]
    all_to_all x3, waiting for transfers between devices: 534 us -> 572 us  [the longest x1 318 us: shards(): lax.all_to_all(jnp.stack(jnp.split(piece, lax.axis_size('virt'), axis=0))...]
    unnamed x16 -> x25, local copies, waits for them, and re-layouts: 44.6 us -> 74.4 us
    squeeze x1 -> x0, local copies, waits for them, and re-layouts: 18.4 us -> none  [shards(): piece = integrals[s]]
  transfers between devices with their start and end apart: 4 -> 4, of which waited for: 4 -> 4; matrix products, arithmetic and copies ran while one was open for 12% -> 13% of each run, Pallas kernels for 0% -> 0%
where the time goes in v1:
time: 1350 us
  waiting for transfers between devices  612 us (45%)
  blocking collectives  372 us (28%)
  local copies, waits for them, and re-layouts  257 us (19%)
  matrix products  59 us (4%)
  starting transfers between devices  20 us (1%)
  between operations  14.2 us (1%)
    all_to_all x1, blocking collectives, shards(): lax.all_to_all(jnp.stack(jnp.split(piece, lax.axis_size('virt'), axis=0))...  372 us
    all_to_all x1, waiting for transfers between devices, shards(): lax.all_to_all(jnp.stack(jnp.split(piece, lax.axis_size('virt'), axis=0))...  318 us
    all_to_all x2, waiting for transfers between devices, shards(): lax.all_to_all(jnp.concatenate(lax.all_to_all(jnp.stack(jnp.split(piece,...  254 us
    reshape x4, local copies, waits for them, and re-layouts, shards(): jnp.concatenate(lax.all_to_all(jnp.stack(jnp.split(piece, lax.axis_size('...  88.5 us
    unnamed x25, local copies, waits for them, and re-layouts  74.4 us
    dot_general x2, matrix products, shards(): jnp.einsum('hrk,ahsk->hras', masked[:, :, s, :], moved, preferred_element...  58.8 us
    reshape x2, local copies, waits for them, and re-layouts, shards(): jnp.transpose(moved, (0, 1, 3, 2, 4))  47.4 us
    unnamed x2, waiting for transfers between devices  39.7 us
  transfers between devices with their start and end apart: 4, of which 4 were waited for; matrix products, arithmetic and copies ran while one was open for 13% of the time, Pallas kernels for 0%

profile of v1, /device:TPU:0, one launch (start us, length us, event | category | flops | bytes accessed | tf_op | source)
XLA Modules:
  0.0 1345.2 jit_solution(14279288042417927330)
XLA Ops:
  7.2 5.1 slice_dynamic-update-slice_fusion.7
  12.3 5.7 slice_dynamic-update-slice_fusion.6
  18.0 5.7 slice_dynamic-update-slice_fusion.5
  23.7 5.6 slice_dynamic-update-slice_fusion.4
  29.3 2.6 slice_dynamic-update-slice_fusion.3
  31.8 2.5 slice_dynamic-update-slice_fusion.2
  34.3 2.6 slice_dynamic-update-slice_fusion.1
  36.9 2.5 slice_dynamic-update-slice_fusion
  39.4 372.0 %all_to_all.40 = bf16[8,64,8,2048]{3,2,1,0:T(8,128)(2,1)} all-to-all(bf16[8,64,8,2048]{3,2,1,0:T(8,128)(2,1)} %get-tuple-element.14), channel_id=1, replica_groups=mesh['virt'=8,'pair'=4] {'virt'}, dimensions={0} | all-to-all | bytes 33554432 | tf_op jit(solution)/shard_map/all_to_all | solution.py:35
  411.4 5.7 all-to-all-start
  417.2 18.6 %copy.45 = bf16[64,8,8,2048]{3,2,0,1:T(8,128)(2,1)} copy(bf16[64,8,8,2048]{3,1,0,2:T(8,128)(2,1)} %bitcast.59) | data formatting | bytes 33554432 | tf_op jit(solution)/shard_map/reshape | solution.py:34
  435.8 25.6 %reshape.242 = bf16[64,8,16384]{2,0,1:T(8,128)(2,1)} reshape(bf16[64,8,8,2048]{3,2,0,1:T(8,128)(2,1)} %copy.45) | data formatting | bytes 33554432 | tf_op jit(solution)/shard_map/reshape | solution.py:34
  461.4 318.3 %all-to-all-done = bf16[8,64,8,2048]{3,2,1,0:T(8,128)(2,1)} async-done(((bf16[8,64,8,2048]{3,2,1,0:T(8,128)(2,1)}), bf16[8,64,8,2048]{3,2,1,0:T(8,128)(2,1)}, u32[]{:S(2)}, u32[]{:S(2)}) %all-to-all-start) | async-done | bytes 16777248 | tf_op jit(solution)/shard_map/all_to_all | solution.py:35
  779.7 7.0 all-to-all-start.3
  786.7 18.6 %copy.44 = bf16[64,8,8,2048]{3,2,0,1:T(8,128)(2,1)} copy(bf16[64,8,8,2048]{3,1,0,2:T(8,128)(2,1)} %bitcast.3) | data formatting | bytes 33554432 | tf_op jit(solution)/shard_map/reshape | solution.py:34
  805.3 25.6 %reshape.241 = bf16[64,8,16384]{2,0,1:T(8,128)(2,1)} reshape(bf16[64,8,8,2048]{3,2,0,1:T(8,128)(2,1)} %copy.44) | data formatting | bytes 33554432 | tf_op jit(solution)/shard_map/reshape | solution.py:34
  831.0 138.7 %all-to-all-done.3 = bf16[64,8,16384]{2,0,1:T(8,128)(2,1)} async-done(((bf16[64,8,16384]{2,0,1:T(8,128)(2,1)}), bf16[64,8,16384]{2,0,1:T(8,128)(2,1)}, u32[]{:S(2)}, u32[]{:S(2)}) %all-to-all-start.3) | async-done | bytes 16777248 | tf_op jit(solution)/shard_map/all_to_all | solution.py:33
  969.7 7.1 all-to-all-start.1
  976.8 0.2 reduce-scatter.4.cloned.1.call-start
  977.0 0.1 reshape.240
  977.1 0.1 dynamic_slice.3
  977.2 0.2 select_reduce_fusion.3
  977.4 0.1 compare_convert_fusion
  977.5 0.1 convert_element_type.16
  977.5 0.9 fusion.2
  978.5 0.1 select_reduce_fusion.1
  978.6 0.1 broadcast_xor_fusion
  978.7 0.1 select_reduce_fusion
  978.8 0.1 iota_compare_fusion.3
  978.9 0.1 iota_compare_fusion
  978.9 0.2 convolution_add_fusion.1
  979.2 0.1 broadcast_and_fusion
  979.3 9.3 copy_multiply_fusion
  988.6 8.0 copy.39
  996.6 10.4 copy.52
  1007.0 14.1 %copy.40 = bf16[64,2,8,4,2048]{4,3,2,0,1:T(4,128)(2,1)} copy(bf16[64,2,8,4,2048]{4,2,0,3,1:T(8,128)(2,1)S(1)} %bitcast.61) | data formatting | bytes 33554432 | tf_op jit(solution)/shard_map/transpose | solution.py:46
  1021.2 23.7 %reshape.235 = bf16[64,2,64,1024]{3,2,0,1:T(8,128)(2,1)} reshape(bf16[64,2,8,4,2048]{4,3,2,0,1:T(4,128)(2,1)} %copy.40) | data formatting | bytes 33554432 | tf_op jit(solution)/shard_map/reshape | solution.py:46
  1044.8 115.0 %all-to-all-done.1 = bf16[64,8,16384]{2,0,1:T(8,128)(2,1)} async-done(((bf16[64,8,16384]{2,0,1:T(8,128)(2,1)}), bf16[64,8,16384]{2,0,1:T(8,128)(2,1)}, u32[]{:S(2)}, u32[]{:S(2)}) %all-to-all-start.1) | async-done | bytes 16777248 | tf_op jit(solution)/shard_map/all_to_all | solution.py:33
  1159.8 8.0 copy.35
  1167.8 10.4 copy.51
  1178.2 14.1 %copy.36 = bf16[64,2,8,4,2048]{4,3,2,0,1:T(4,128)(2,1)} copy(bf16[64,2,8,4,2048]{4,2,0,3,1:T(8,128)(2,1)S(1)} %bitcast.63) | data formatting | bytes 33554432 | tf_op jit(solution)/shard_map/transpose | solution.py:46
  1192.3 23.7 %reshape.231 = bf16[64,2,64,1024]{3,2,0,1:T(8,128)(2,1)} reshape(bf16[64,2,8,4,2048]{4,3,2,0,1:T(4,128)(2,1)} %copy.36) | data formatting | bytes 33554432 | tf_op jit(solution)/shard_map/reshape | solution.py:46
  1216.1 26.7 %fusion.1 = f32[2,1024,64,64]{1,3,2,0:T(8,128)} fusion(bf16[64,2,64,1024]{3,2,0,1:T(8,128)(2,1)} %reshape.231, bf16[2,1024,2,1024]{3,1,0,2:T(8,128)(2,1)} %copy_multiply_fusion), kind=kOutput, calls=%fused_computation.7 | convolution fusion | flops 17179869184 | bytes 54525952 | tf_op jit(solution)/shard_map/hrk,ahsk->hras/dot_general | solution.py:47
  1242.8 32.1 %multiply_reduce_fusion = (f32[2,1024]{1,0:T(2,128)S(1)}, bf16[2,1024,64,64]{1,3,2,0:T(8,128)(2,1)}) fusion(f32[2,1024]{1,0:T(2,128)S(1)} %bitcast.67, f32[2,64,64]{2,1,0:T(8,128)S(1)} %convolution_add_fusion.1, pred[2,64,64]{2,1,0:T(8,128)(4,1)S(1)} %iota_compare_fusion, pred[2,1024,64]{1,2,0:T(8,128)(4,1)S(1)} %broadcast_and_fusion, ...), kind=kOutput, calls=%fused_computation | convolution fusion | flops 17246976000 | bytes 71491584 | tf_op jit(solution)/shard_map/hrk,ahsk->hras/dot_general | solution.py:47
  1274.9 1.0 copy.46
  1275.9 21.2 %copy.41 = bf16[2,1024,4096]{2,1,0:T(8,128)(2,1)} copy(bf16[2,1024,4096]{1,2,0:T(8,128)(2,1)} %bitcast.64) | data formatting | bytes 33554432
  1297.2 39.7 %reduce-scatter.4.cloned.1.call-done = f32[128,2]{1,0:T(8,128)} async-done(((f32[1024,2]{1,0:T(8,128)}), f32[128,2]{1,0:T(8,128)}) %reduce-scatter.4.cloned.1.call-update) | async-done | bytes 1040
  1336.8 1.5 copy.47
  (20 shorter events, 0.1 us)
Async XLA Ops:
  7.2 22.1 %copy-start = (bf16[2,512,8,2048]{3,2,1,0:T(8,128)(2,1)S(1)}, bf16[2,512,8,2048]{3,2,1,0:T(8,128)(2,1)}, u32[]{:S(2)}) copy-start(bf16[2,512,8,2048]{3,2,1,0:T(8,128)(2,1)} %param.8) | copy-start | bytes 100663296
  411.4 368.3 %all-to-all-start = ((bf16[8,64,8,2048]{3,2,1,0:T(8,128)(2,1)}), bf16[8,64,8,2048]{3,2,1,0:T(8,128)(2,1)}, u32[]{:S(2)}, u32[]{:S(2)}) async-start(bf16[8,64,8,2048]{3,2,1,0:T(8,128)(2,1)} %get-tuple-element.15), calls=%async_computation | async-start | bytes 33554432 | tf_op jit(solution)/shard_map/all_to_all | solution.py:35
  779.7 190.0 %all-to-all-start.3 = ((bf16[64,8,16384]{2,0,1:T(8,128)(2,1)}), bf16[64,8,16384]{2,0,1:T(8,128)(2,1)}, u32[]{:S(2)}, u32[]{:S(2)}) async-start(bf16[64,8,16384]{2,0,1:T(8,128)(2,1)} %reshape.242), calls=%async_computation.3 | async-start | bytes 33554432 | tf_op jit(solution)/shard_map/all_to_all | solution.py:33
  830.9 146.1 %copy-start.2 = (f32[512]{0:T(512)S(1)}, f32[512]{0:T(512)}, u32[]{:S(2)}) copy-start(f32[512]{0:T(512)} %param.13) | copy-start | bytes 6148
  830.9 146.2 %copy-start.3 = (s32[8]{0:T(128)S(1)}, s32[8]{0:T(128)}, u32[]{:S(2)}) copy-start(s32[8]{0:T(128)} %param.9) | copy-start | bytes 100
  831.0 146.2 %copy-start.5 = (s32[8]{0:T(128)S(1)}, s32[8]{0:T(128)}, u32[]{:S(2)}) copy-start(s32[8]{0:T(128)} %param.10) | copy-start | bytes 100
  831.0 146.6 %copy-start.1 = (s32[2,1024,2]{1,2,0:T(2,128)S(1)}, s32[2,1024,2]{1,2,0:T(2,128)}, u32[]{:S(2)}) copy-start(s32[2,1024,2]{1,2,0:T(2,128)} %param.11) | copy-start | bytes 49156
  831.0 146.6 %copy-start.4 = (f32[100]{0:T(128)S(1)}, f32[100]{0:T(128)}, u32[]{:S(2)}) copy-start(f32[100]{0:T(128)} %param.12) | copy-start | bytes 1204
  969.7 190.1 %all-to-all-start.1 = ((bf16[64,8,16384]{2,0,1:T(8,128)(2,1)}), bf16[64,8,16384]{2,0,1:T(8,128)(2,1)}, u32[]{:S(2)}, u32[]{:S(2)}) async-start(bf16[64,8,16384]{2,0,1:T(8,128)(2,1)} %reshape.241), calls=%async_computation.1 | async-start | bytes 33554432 | tf_op jit(solution)/shard_map/all_to_all | solution.py:33
  976.8 360.1 %reduce-scatter.4.cloned.1.call-start = ((), (), s32[]{:S(2)}) async-start(), calls=%async_computation.5 | async-start | bytes 589824
Sparse Core Ops, SparseCore 0:
  1276.0 60.7 reduce-scatter.3
